TPU v7x, 32 devices: a whole 2x2x4 slice. The times are simulated.
32 devices in a mesh: dp: 4 (over x, core), tensor: 8 (over z, y).
Axes of the slice: x: 2, y: 2, z: 4, core: 2. Of those that a mesh axis runs over, the one named last changes fastest.
Arguments:
- tokens: bfloat16 [8192, 1024], P('dp'), may hold values from -6 to 6
- segment_ids: int32 [4, 2048], P('dp'), may hold values from 0 to 7, never falling along the last dimension, each value on 1 to 512 neighbouring positions
- first_gain: bfloat16 [1024], replicated, may hold values from 0.5 to 1.5
- first_shift: bfloat16 [1024], replicated, may hold values from -3 to 3
- qkv_weight: bfloat16 [1024, 16, 192], P(None, 'tensor'), may hold values from -0.1875 to 0.1875
- qv_bias: bfloat16 [16, 128], P('tensor'), may hold values from -3 to 3
- out_weight: bfloat16 [1024, 1024], P('tensor'), may hold values from -0.5 to 0.5
- out_bias: bfloat16 [1024], replicated, may hold values from -2 to 2
- second_gain: bfloat16 [1024], replicated, may hold values from 0.5 to 1.5
- second_shift: bfloat16 [1024], replicated, may hold values from -3 to 3
- up_weight: bfloat16 [1024, 4096], P(None, 'tensor'), may hold values from -0.1875 to 0.1875
- up_bias: bfloat16 [4096], P('tensor'), may hold values from -3 to 3
- down_weight: bfloat16 [4096, 1024], P('tensor'), may hold values from -0.125 to 0.125
- down_bias: bfloat16 [1024], replicated, may hold values from -2 to 2
- cotangent: bfloat16 [8192, 1024], P('dp'), may hold values from -6 to 6
Outputs:
- output: bfloat16 [8192, 1024], P('dp')
- grad_tokens: bfloat16 [8192, 1024], P('dp')
- grad_first_gain: float32 [1024], replicated
- grad_first_shift: float32 [1024], replicated
- grad_qkv_weight: float32 [1024, 16, 192], P(None, 'tensor')
- grad_qv_bias: float32 [16, 128], P('tensor')
- grad_out_weight: float32 [1024, 1024], P('tensor')
- grad_out_bias: float32 [1024], replicated
- grad_second_gain: float32 [1024], replicated
- grad_second_shift: float32 [1024], replicated
- grad_up_weight: float32 [1024, 4096], P(None, 'tensor')
- grad_up_bias: float32 [4096], P('tensor')
- grad_down_weight: float32 [4096, 1024], P('tensor')
- grad_down_bias: float32 [1024], replicated
Inputs may be any that keep to these rules, and one draw needn't show every extreme that they name: `segment_ids`: each row of 2048 positions is cut into documents of consecutive positions, at most 512 long, one exactly that long; ids never fall along a row.
All inputs are finite; a program needn't handle non-finite values.
Results may differ from a plain program's by a relative error of at most 0.023.
Values may be sent and summed in bfloat16 or wider, within the bound.
A program may use at most 128 MiB of HBM per device.

v0:
```python
import math
import jax
import jax.numpy as jnp
from jax import lax
from jax.sharding import PartitionSpec as P

norm_eps = 1e-05


def layer_norm(values, gain_vec, shift_vec):
    center = jnp.mean(values, axis=-1, keepdims=True)
    offset = values - center
    spread = jnp.mean(offset * offset, axis=-1, keepdims=True)
    return offset * lax.rsqrt(spread + norm_eps) * gain_vec + shift_vec


def gelu_tanh(values):
    return (
        0.5
        * values
        * (1.0 + jnp.tanh(0.7978845608028654 * (values + 0.044715 * values * values * values)))
    )


def head_slopes(local_heads):
    total = local_heads * lax.axis_size("tensor")
    first = lax.axis_index("tensor") * local_heads
    heads_idx = first + jnp.arange(local_heads, dtype=jnp.int32)
    return jnp.exp2(-8.0 * (heads_idx + 1).astype(jnp.float32) / total)


def block_scores(query_blk, keys, start, seg_row, slopes):
    rows = query_blk.shape[0]
    length = keys.shape[0]
    scale = 1.0 / math.sqrt(keys.shape[2])
    raw = jnp.einsum("qhe,khe->hqk", query_blk, keys, preferred_element_type=jnp.float32) * scale
    query_pos = start + jnp.arange(rows, dtype=jnp.int32)
    key_pos = jnp.arange(length, dtype=jnp.int32)
    distance = (query_pos[:, None] - key_pos[None, :]).astype(jnp.float32)
    raw = raw - slopes[:, None, None] * distance[None]
    query_seg = lax.dynamic_slice_in_dim(seg_row, start, rows, 0)
    allowed = (query_seg[:, None] == seg_row[None, :]) & (key_pos[None, :] <= query_pos[:, None])
    return jnp.where(allowed[None], raw, -1e30)


def attend_forward(query, keys, values, seg_row, slopes):
    length = query.shape[0]
    block = min(512, length)

    def one_block(index):
        start = index * block
        query_blk = lax.dynamic_slice_in_dim(query, start, block, 0)
        scores = block_scores(query_blk, keys, start, seg_row, slopes)
        peak = jnp.max(scores, axis=-1, keepdims=True)
        expo = jnp.exp(scores - peak)
        total = jnp.sum(expo, axis=-1, keepdims=True)
        weights_low = (expo / total).astype(jnp.bfloat16)
        ctx_blk = jnp.einsum(
            "hqk,khe->qhe", weights_low, values, preferred_element_type=jnp.float32
        )
        return (ctx_blk, (peak + jnp.log(total))[:, :, 0])

    ctx_blocks, lse_blocks = lax.map(one_block, jnp.arange(length // block, dtype=jnp.int32))
    return (ctx_blocks.reshape(query.shape), lse_blocks)


def attend_backward(query, keys, values, seg_row, slopes, lse_blocks, grad_context):
    length = query.shape[0]
    block = min(512, length)
    scale = 1.0 / math.sqrt(keys.shape[2])

    def one_block(carry, index):
        grad_keys, grad_values = carry
        start = index * block
        query_blk = lax.dynamic_slice_in_dim(query, start, block, 0)
        grad_blk = lax.dynamic_slice_in_dim(grad_context, start, block, 0)
        scores = block_scores(query_blk, keys, start, seg_row, slopes)
        probs = jnp.exp(scores - lse_blocks[index][:, :, None])
        probs_low = probs.astype(jnp.bfloat16)
        grad_probs = jnp.einsum(
            "qhe,khe->hqk", grad_blk, values, preferred_element_type=jnp.float32
        )
        inner = jnp.sum(probs * grad_probs, axis=-1, keepdims=True)
        grad_scores = (probs * (grad_probs - inner)).astype(jnp.bfloat16)
        grad_query = (
            jnp.einsum("hqk,khe->qhe", grad_scores, keys, preferred_element_type=jnp.float32)
            * scale
        )
        grad_keys = (
            grad_keys
            + jnp.einsum("hqk,qhe->khe", grad_scores, query_blk, preferred_element_type=jnp.float32)
            * scale
        )
        grad_values = grad_values + jnp.einsum(
            "hqk,qhe->khe", probs_low, grad_blk, preferred_element_type=jnp.float32
        )
        return ((grad_keys, grad_values), grad_query)

    empty = jnp.zeros(keys.shape, jnp.float32)
    (grad_keys, grad_values), grad_query = lax.scan(
        one_block, (empty, empty), jnp.arange(length // block, dtype=jnp.int32)
    )
    return (grad_query.reshape(query.shape), grad_keys, grad_values)


def attn_front(
    tokens_f, seg_row, first_gain, first_shift, qkv_weight, qv_bias, out_weight, out_bias
):
    length = tokens_f.shape[0]
    normed_low = layer_norm(
        tokens_f, first_gain.astype(jnp.float32), first_shift.astype(jnp.float32)
    ).astype(jnp.bfloat16)
    merged = jnp.einsum("td,dhe->the", normed_low, qkv_weight, preferred_element_type=jnp.float32)
    width = merged.shape[2] // 3
    bias_f = qv_bias.astype(jnp.float32)
    query = (merged[:, :, :width] + bias_f[:, :width]).astype(jnp.bfloat16)
    keys = merged[:, :, width : 2 * width].astype(jnp.bfloat16)
    values = (merged[:, :, 2 * width :] + bias_f[:, width:]).astype(jnp.bfloat16)
    slopes = head_slopes(query.shape[1])
    context, lse_blocks = attend_forward(query, keys, values, seg_row, slopes)
    context_low = context.reshape(length, -1).astype(jnp.bfloat16)
    partial_out = jnp.dot(context_low, out_weight, preferred_element_type=jnp.float32).astype(
        jnp.bfloat16
    )
    mixed = lax.psum(partial_out, "tensor").astype(jnp.float32)
    middle = tokens_f + mixed + out_bias.astype(jnp.float32)
    return (normed_low, query, keys, values, context_low, lse_blocks, middle, slopes)


def mlp_front(middle, second_gain, second_shift, up_weight, up_bias):
    second_low = layer_norm(
        middle, second_gain.astype(jnp.float32), second_shift.astype(jnp.float32)
    ).astype(jnp.bfloat16)
    upper = jnp.dot(second_low, up_weight, preferred_element_type=jnp.float32) + up_bias.astype(
        jnp.float32
    )
    hidden_low = gelu_tanh(upper).astype(jnp.bfloat16)
    return (second_low, upper, hidden_low)


def norm_pull(values, gain_vec, shift_vec, grad_norm):
    norm_value, pull_fn = jax.vjp(
        layer_norm, values, gain_vec.astype(jnp.float32), shift_vec.astype(jnp.float32)
    )
    return pull_fn(grad_norm)


def per_device(
    tokens,
    segment_ids,
    first_gain,
    first_shift,
    qkv_weight,
    qv_bias,
    out_weight,
    out_bias,
    second_gain,
    second_shift,
    up_weight,
    up_bias,
    down_weight,
    down_bias,
    cotangent,
):
    tokens_f = tokens.astype(jnp.float32)
    seg_row = segment_ids[0]
    saved = attn_front(
        tokens_f, seg_row, first_gain, first_shift, qkv_weight, qv_bias, out_weight, out_bias
    )
    middle = saved[6]
    second_low, upper, hidden_low = mlp_front(middle, second_gain, second_shift, up_weight, up_bias)
    part_down = jnp.dot(hidden_low, down_weight, preferred_element_type=jnp.float32).astype(
        jnp.bfloat16
    )
    feed = lax.psum(part_down, "tensor").astype(jnp.float32)
    output = (middle + feed + down_bias.astype(jnp.float32)).astype(jnp.bfloat16)
    normed_low, query, keys, values, context_low, lse_blocks, middle, slopes = saved
    grad_out = cotangent.astype(jnp.float32)
    grad_down_weight = jnp.einsum(
        "tf,td->fd", hidden_low, cotangent, preferred_element_type=jnp.float32
    )
    grad_down_bias = jnp.sum(grad_out, axis=0)
    grad_hidden = jnp.einsum(
        "td,fd->tf", cotangent, down_weight, preferred_element_type=jnp.float32
    )
    gelu_value, gelu_pull = jax.vjp(gelu_tanh, upper)
    grad_upper_low = gelu_pull(grad_hidden)[0].astype(jnp.bfloat16)
    grad_up_bias = jnp.sum(grad_upper_low.astype(jnp.float32), axis=0)
    grad_up_weight = jnp.einsum(
        "td,tf->df", second_low, grad_upper_low, preferred_element_type=jnp.float32
    )
    part_second = jnp.einsum(
        "tf,df->td", grad_upper_low, up_weight, preferred_element_type=jnp.float32
    )
    grad_second = lax.psum(part_second.astype(jnp.bfloat16), "tensor").astype(jnp.float32)
    grad_middle_norm, grad_second_gain, grad_second_shift = norm_pull(
        middle, second_gain, second_shift, grad_second
    )
    grad_middle = grad_out + grad_middle_norm
    mlp_grads = (
        lax.psum(grad_down_weight.astype(jnp.bfloat16), "dp").astype(jnp.float32),
        lax.psum(grad_up_weight.astype(jnp.bfloat16), "dp").astype(jnp.float32),
        lax.psum(grad_up_bias.astype(jnp.bfloat16), "dp").astype(jnp.float32),
        lax.psum(grad_down_bias.astype(jnp.bfloat16), "dp").astype(jnp.float32),
        lax.psum(grad_second_gain.astype(jnp.bfloat16), "dp").astype(jnp.float32),
        lax.psum(grad_second_shift.astype(jnp.bfloat16), "dp").astype(jnp.float32),
    )
    grad_middle_low = grad_middle.astype(jnp.bfloat16)
    grad_out_bias = jnp.sum(grad_middle, axis=0)
    grad_out_weight = jnp.einsum(
        "tc,td->cd", context_low, grad_middle_low, preferred_element_type=jnp.float32
    )
    grad_context = jnp.einsum(
        "td,cd->tc", grad_middle_low, out_weight, preferred_element_type=jnp.float32
    )
    grad_context = grad_context.astype(jnp.bfloat16).reshape(query.shape)
    grad_query, grad_keys, grad_values = attend_backward(
        query, keys, values, seg_row, slopes, lse_blocks, grad_context
    )
    grad_query_low = grad_query.astype(jnp.bfloat16)
    grad_values_low = grad_values.astype(jnp.bfloat16)
    grad_merged = jnp.concatenate(
        [grad_query_low, grad_keys.astype(jnp.bfloat16), grad_values_low], axis=2
    )
    grad_qv_bias = jnp.concatenate(
        [
            jnp.sum(grad_query_low.astype(jnp.float32), axis=0),
            jnp.sum(grad_values_low.astype(jnp.float32), axis=0),
        ],
        axis=1,
    )
    grad_qkv_weight = jnp.einsum(
        "td,the->dhe", normed_low, grad_merged, preferred_element_type=jnp.float32
    )
    part_first = jnp.einsum(
        "the,dhe->td", grad_merged, qkv_weight, preferred_element_type=jnp.float32
    )
    grad_first = lax.psum(part_first.astype(jnp.bfloat16), "tensor").astype(jnp.float32)
    grad_tokens_norm, grad_first_gain, grad_first_shift = norm_pull(
        tokens_f, first_gain, first_shift, grad_first
    )
    grad_tokens_f = grad_middle + grad_tokens_norm
    grad_tokens = grad_tokens_f.astype(jnp.bfloat16)
    attn_grads = (
        lax.psum(grad_qkv_weight.astype(jnp.bfloat16), "dp").astype(jnp.float32),
        lax.psum(grad_qv_bias.astype(jnp.bfloat16), "dp").astype(jnp.float32),
        lax.psum(grad_out_weight.astype(jnp.bfloat16), "dp").astype(jnp.float32),
        lax.psum(grad_out_bias.astype(jnp.bfloat16), "dp").astype(jnp.float32),
        lax.psum(grad_first_gain.astype(jnp.bfloat16), "dp").astype(jnp.float32),
        lax.psum(grad_first_shift.astype(jnp.bfloat16), "dp").astype(jnp.float32),
    )
    return (
        output,
        grad_tokens,
        attn_grads[4],
        attn_grads[5],
        attn_grads[0],
        attn_grads[1],
        attn_grads[2],
        attn_grads[3],
        mlp_grads[4],
        mlp_grads[5],
        mlp_grads[1],
        mlp_grads[2],
        mlp_grads[0],
        mlp_grads[3],
    )


def solution(mesh):
    return jax.shard_map(
        per_device,
        mesh=mesh,
        in_specs=(
            P("dp", None),
            P("dp", None),
            P(),
            P(),
            P(None, "tensor", None),
            P("tensor", None),
            P("tensor", None),
            P(),
            P(),
            P(),
            P(None, "tensor"),
            P("tensor"),
            P("tensor", None),
            P(),
            P("dp", None),
        ),
        out_specs=(
            P("dp", None),
            P("dp", None),
            P(),
            P(),
            P(None, "tensor", None),
            P("tensor", None),
            P("tensor", None),
            P(),
            P(),
            P(),
            P(None, "tensor"),
            P("tensor"),
            P("tensor", None),
            P(),
        ),
        check_vma=False,
    )
```

profile of v0, /device:TPU:0, one launch (start us, length us, event | category | flops | bytes accessed | tf_op | source)
XLA Modules:
  0.0 955.8 jit_solution(13853205372670522851)
XLA Ops:
  9.8 2.8 convert_reduce_fusion
  21.4 48.7 %while.28 = (s32[]{:T(128)}, bf16[4,512,2,64]{1,3,2,0:T(8,128)(2,1)S(1)}, f32[4,2,512]{2,1,0:T(2,128)S(1)}, s32[4]{0:T(128)S(1)}, s32[2048]{0:T(1024)S(1)}, /*in...) while((s32[]{:T(128)}, ...), condition=%wide.region_5.6_spmd.clone, body=%wide.region_2.5_spmd.clone.sunk | while | flops 579862016 | bytes 47633644 | solution.py:63
  27.1 3.2 fusion.131
  30.3 3.2 fusion.132
  39.3 3.2 fusion.131
  42.5 3.2 fusion.132
  51.4 3.2 fusion.131
  54.6 3.2 fusion.132
  60.8 2.8 fusion.130
  63.5 3.2 fusion.131
  66.7 3.2 fusion.132
  70.7 3.3 convolution_convert_fusion.2
  74.8 158.6 %all-reduce.8.cloned.1.call-done = bf16[2048,1024]{1,0:T(8,128)(2,1)} async-done(((bf16[2048,1024]{1,0:T(8,128)(2,1)}), bf16[2048,1024]{1,0:T(8,128)(2,1)}) %all-reduce.8.cloned.1.call-update) | async-done | bytes 4194320 | tf_op jit(solution)/shard_map/psum | solution.py:125
  233.3 5.0 fusion.54
  241.4 3.5 fusion.73
  244.9 6.4 fusion.76
  252.7 4.4 convolution_convert_fusion
  257.4 7.1 convolution_convert_fusion.4
  265.3 4.5 convolution_convert_fusion.5
  269.8 142.9 %all-reduce.10.cloned.1.call-done = bf16[2048,1024]{1,0:T(8,128)(2,1)} async-done(((bf16[2048,1024]{1,0:T(8,128)(2,1)}), bf16[2048,1024]{1,0:T(8,128)(2,1)}) %all-reduce.10.cloned.1.call-update) | async-done | bytes 4194320 | tf_op jit(solution)/shard_map/psum | solution.py:195
  412.7 6.8 fusion.47
  421.0 6.9 fusion.48
  427.9 5.7 fusion.78
  440.1 117.1 %while.29 = (s32[]{:T(128)}, f32[2048,2,64]{0,2,1:T(8,128)S(1)}, f32[2048,2,64]{0,2,1:T(8,128)}, bf16[4,512,2,64]{1,3,2,0:T(8,128)(2,1)}, s32[4]{0:T(128)S(1)}, ...) while((s32[]{:T(128)}, f32[2048,2,64]{0,2,1:T(8,128)S(1)}, ...), condition=%wide.region_15.16_spmd.clone, body=%wide.region_13.15_spmd.clone.sunk | while | flops 1371864576 | bytes 145007648 | solution.py:100
  447.6 6.2 multiply_reduce_fusion.3
  453.8 8.7 multiply_convert_fusion.5
  462.5 4.6 fusion.145
  476.8 6.2 multiply_reduce_fusion.3
  483.0 8.7 multiply_convert_fusion.5
  491.7 4.6 fusion.145
  505.9 6.2 multiply_reduce_fusion.3
  512.2 8.7 multiply_convert_fusion.5
  520.8 4.6 fusion.145
  535.1 6.2 multiply_reduce_fusion.3
  541.3 8.7 multiply_convert_fusion.5
  550.0 4.6 fusion.145
  563.2 7.1 convolution_convert_fusion.1
  570.3 4.4 bitcast_convert_fusion
  574.7 3.0 reduce_sum.218
  577.7 2.9 reduce_sum.213
  580.9 49.7 %all-reduce.14.cloned.1.call-done = (bf16[1024,2,192]{0,2,1:T(8,128)(2,1)}, bf16[128,1024]{1,0:T(8,128)(2,1)}, bf16[1024,512]{1,0:T(8,128)(2,1)}, bf16[512,1024]{1,0:T(8,128)(2,1)}) async-done(((bf16[1024,2,192]{0,2,1:T(8,128)(2,1)}, bf16[128,1024]{1,0:T(8,128)(2,1)}, bf16[1024,512]{1,0:T(8,128)(2,1)}, bf16[512,1024]{1,0:T(8,128)(2,1)}), (bf16[1024,2,192]{0,2,1:T(8,128)(2,1)}, bf16[128,1024]{1,0:T(8,128)(2,1)}, ...) | async-done | bytes 3145744 | tf_op jit(solution)/shard_map/psum | solution.py:245
  634.9 2.8 convert_element_type.253
  639.3 265.9 %all-reduce.12.cloned.1.call-done = (bf16[2048,1024]{1,0:T(8,128)(2,1)}, bf16[2048,1024]{1,0:T(8,128)(2,1)}) async-done(((bf16[2048,1024]{1,0:T(8,128)(2,1)}, bf16[2048,1024]{1,0:T(8,128)(2,1)}), (bf16[2048,1024]{1,0:T(8,128)(2,1)}, bf16[2048,1024]{1,0:T(8,128)(2,1)})) %all-reduce.12.cloned.1.call-update) | async-done | bytes 8388624 | tf_op jit(solution)/shard_map/psum | solution.py:175
  905.2 4.5 fusion.51
  909.7 2.9 reduce_sum.205
  912.7 6.8 fusion.49
  919.5 10.8 %all-reduce.1 = (bf16[1024]{0:T(1024)(128)(2,1)S(1)}, bf16[1024]{0:T(1024)(128)(2,1)S(1)}, bf16[2,128]{1,0:T(2,128)(2,1)S(1)}, bf16[1024]{0:T(1024)(128)(2,1)S(1...) all-reduce(bf16[1024]{0:T(1024)(128)(2,1)S(1)} %get-tuple-element.2, ...), channel_id=1, replica_groups=mesh['dp'=4,'tensor'=8] {'dp'}, use_global_device_ids=true, to_apply=%region_20.21 | all-reduce | flops 6912 | bytes 27648 | tf_op jit(solution)/shard_map/psum | solution.py:249
  935.0 14.1 %add_convert_fusion = (bf16[2048,1024]{1,0:T(8,128)(2,1)}, bf16[2048,1024]{1,0:T(8,128)(2,1)}) fusion(f32[2048,1024]{1,0:T(8,128)} %copy-done.10, bf16[2048,1024]{1,0:T(8,128)(2,1)} %param.19, bf16[2048,1024]{1,0:T(8,128)(2,1)} %get-tuple-element.260, f32[2048]{0:T(1024)S(1)} %negate_multiply_fusion, f32[2048]{0:T(1024)S(1)} %multiply_multiply_fusion.2, ...), kind=kLoop, calls=%fused_computation.75 | loop fusion | flops 37748736 | bytes 33599488 | tf_op jit(solution)/shard_map/convert_element_type | solution.py:243
  (283 shorter events, 88.0 us)
Async XLA Ops:
  7.2 237.7 %copy-start = (bf16[512,1024]{1,0:T(8,128)(2,1)S(1)}, bf16[512,1024]{1,0:T(8,128)(2,1)}, u32[]{:S(2)}) copy-start(bf16[512,1024]{1,0:T(8,128)(2,1)} %param.31) | copy-start | bytes 3145732
  7.2 226.1 %all-reduce.8.cloned.1.call-start = ((), (), s32[]{:S(2)}) async-start(), calls=%async_computation | async-start | bytes 8388608 | tf_op jit(solution)/shard_map/psum | solution.py:125
  7.3 5.4 copy-start.3
  9.1 5.0 copy-start.35
  21.4 49.3 %copy-start.28 = (bf16[128,1024]{1,0:T(8,128)(2,1)S(1)}, bf16[128,1024]{1,0:T(8,128)(2,1)}, u32[]{:S(2)}) copy-start(bf16[128,1024]{1,0:T(8,128)(2,1)} %param.25) | copy-start | bytes 786436
  70.2 3.9 copy-start.16
  74.1 338.6 %all-reduce.10.cloned.1.call-start = ((), (), s32[]{:S(2)}) async-start(), calls=%async_computation.1 | async-start | bytes 8388608 | tf_op jit(solution)/shard_map/psum | solution.py:195
  74.7 182.7 %copy-start.45 = (f32[512]{0:T(512)}, f32[512]{0:T(512)S(1)}, u32[]{:S(2)}) copy-start(f32[512]{0:T(512)S(1)} %convert_element_type.218) | copy-start | bytes 6148
  74.7 353.2 %copy-start.31 = (f32[1024]{0:T(1024)}, f32[1024]{0:T(1024)S(1)}, u32[]{:S(2)}) copy-start(f32[1024]{0:T(1024)S(1)} %convert_element_type.214) | copy-start | bytes 12292
  233.3 5.0 copy-start.4
  233.3 5.9 copy-start.7
  241.4 3.5 copy-start.14
  244.9 6.4 copy-start.54
  257.1 373.4 %all-reduce.14.cloned.1.call-start = ((), (), s32[]{:S(2)}) async-start(), calls=%async_computation.3 | async-start | bytes 6291456 | tf_op jit(solution)/shard_map/psum | solution.py:245
  257.4 7.1 copy-start.5
  257.4 7.1 copy-start.8
  257.4 7.9 copy-start.53
  412.7 6.8 copy-start.6
  412.7 7.1 copy-start.9
  412.7 8.3 copy-start.11
  421.0 6.9 copy-start.15
  427.9 5.7 copy-start.19
  447.6 6.2 copy-start.1
  453.8 8.7 copy-start.12
  462.5 4.6 copy-start.2
  462.5 4.8 copy-start.20
  476.8 6.2 copy-start.1
  483.0 8.7 copy-start.12
  491.7 4.6 copy-start.2
  491.7 4.8 copy-start.20
  505.9 6.2 copy-start.1
  512.2 8.7 copy-start.12
  520.8 4.6 copy-start.2
  520.8 4.8 copy-start.20
  535.1 6.2 copy-start.1
  541.3 8.7 copy-start.12
  550.0 4.6 copy-start.2
  550.0 4.8 copy-start.20
  562.9 7.4 copy-start.51
  562.9 342.3 %all-reduce.12.cloned.1.call-start = ((), (), s32[]{:S(2)}) async-start(), calls=%async_computation.2 | async-start | bytes 16777216 | tf_op jit(solution)/shard_map/psum | solution.py:175
  574.7 5.9 copy-start.22
  630.6 7.2 copy-start.27
  632.5 272.8 %copy-start.30 = (f32[2048]{0:T(1024)S(1)}, f32[2048]{0:T(1024)}, u32[]{:S(2)}) copy-start(f32[2048]{0:T(1024)} %copy-done.29) | copy-start | bytes 24580
  632.5 272.8 %copy-start.36 = (f32[1024]{0:T(1024)S(1)}, f32[1024]{0:T(1024)}, u32[]{:S(2)}) copy-start(f32[1024]{0:T(1024)} %copy-done.35) | copy-start | bytes 12292
  912.6 6.9 copy-start.39
  912.6 6.9 copy-start.40
  912.6 6.8 copy-start.48
  912.7 22.3 %copy-start.32 = (f32[1024]{0:T(1024)S(1)}, f32[1024]{0:T(1024)}, u32[]{:S(2)}) copy-start(f32[1024]{0:T(1024)} %copy-done.31) | copy-start | bytes 12292
  (32 other events, 64.1 us)
Sparse Core Ops, SparseCore 0:
  74.2 159.0 all-reduce.7
  257.2 155.3 all-reduce.9
  563.0 67.4 all-reduce.13
  635.1 270.0 all-reduce.11
where the time goes:
time: 964 us; the launch traced here: 956 us
  waiting for transfers between devices  617 us (64%)
  other arithmetic  146 us (15%)
  matrix products  134 us (14%)
  local copies, waits for them, and re-layouts  18.3 us (2%)
  between operations  14.6 us (2%)
  loops' own time  14.3 us (1%)
  blocking collectives  10.8 us (1%)
    psum x1, waiting for transfers between devices, per_device(): feed = lax.psum(part_down, 'tensor').astype(jnp.float32)  266 us
    psum x1, waiting for transfers between devices, attn_front(): mixed = lax.psum(partial_out, 'tensor').astype(jnp.float32)  159 us
    psum x1, waiting for transfers between devices, per_device(): lax.psum(part_second.astype(jnp.bfloat16), 'tensor').astype(jnp.float32)  143 us
    psum x1, waiting for transfers between devices, per_device(): lax.psum(grad_qkv_weight.astype(jnp.bfloat16), 'dp').astype(jnp.float32)  49.7 us
    dot_general x8, matrix products, block_scores(): jnp.einsum('qhe,khe->hqk', query_blk, keys, preferred_element_type=jnp.fl...  36 us
    convert_element_type x4, other arithmetic, one_block(): grad_scores = (probs * (grad_probs - inner)).astype(jnp.bfloat16)  34.7 us
    reduce_sum x6, other arithmetic, layer_norm(): return offset * lax.rsqrt(spread + norm_eps) * gain_vec + shift_vec  30.7 us
  transfers between devices with their start and end apart: 4, of which 4 were waited for; matrix products, arithmetic and copies ran while one was open for 4% of the time, Pallas kernels for 0%

commit v1 on v0

--- a/solution.py
+++ b/solution.py
@@ -242,7 +242,9 @@
     grad_tokens_f = grad_middle + grad_tokens_norm
     grad_tokens = grad_tokens_f.astype(jnp.bfloat16)
     attn_grads = (
-        lax.psum(grad_qkv_weight.astype(jnp.bfloat16), "dp").astype(jnp.float32),
+        jnp.sum(lax.all_gather(grad_qkv_weight.astype(jnp.bfloat16), "dp"), axis=0).astype(
+            jnp.float32
+        ),
         lax.psum(grad_qv_bias.astype(jnp.bfloat16), "dp").astype(jnp.float32),
         lax.psum(grad_out_weight.astype(jnp.bfloat16), "dp").astype(jnp.float32),
         lax.psum(grad_out_bias.astype(jnp.bfloat16), "dp").astype(jnp.float32),

time: 964 us -> 930 us (0.965)
  waiting for transfers between devices: 617 us -> 566 us
    psum x1, waiting for transfers between devices: 49.7 us -> 0.01 us  [per_device(): lax.psum(grad_out_weight.astype(jnp.bfloat16), 'dp').astype(jnp.float32)]
  transfers between devices with their start and end apart: 4 -> 5, of which waited for: 4 -> 4; matrix products, arithmetic and copies ran while one was open for 4% -> 17% of each run, Pallas kernels for 0% -> 0%
where the time goes in v1:
time: 930 us; the launch traced here: 921 us
  waiting for transfers between devices  566 us (61%)
  other arithmetic  151 us (16%)
  matrix products  137 us (15%)
  local copies, waits for them, and re-layouts  26.4 us (3%)
  between operations  14.8 us (2%)
  loops' own time  13.9 us (1%)
  blocking collectives  10.8 us (1%)
    psum x1, waiting for transfers between devices, per_device(): feed = lax.psum(part_down, 'tensor').astype(jnp.float32)  261 us
    psum x1, waiting for transfers between devices, attn_front(): mixed = lax.psum(partial_out, 'tensor').astype(jnp.float32)  159 us
    psum x1, waiting for transfers between devices, per_device(): lax.psum(part_second.astype(jnp.bfloat16), 'tensor').astype(jnp.float32)  143 us
    dot_general x8, matrix products, block_scores(): jnp.einsum('qhe,khe->hqk', query_blk, keys, preferred_element_type=jnp.fl...  36 us
    convert_element_type x4, other arithmetic, one_block(): grad_scores = (probs * (grad_probs - inner)).astype(jnp.bfloat16)  35 us
    reduce_sum x6, other arithmetic, layer_norm(): return offset * lax.rsqrt(spread + norm_eps) * gain_vec + shift_vec  30.8 us
  transfers between devices with their start and end apart: 5, of which 4 were waited for; matrix products, arithmetic and copies ran while one was open for 17% of the time, Pallas kernels for 0%

profile of v1, /device:TPU:0, one launch (start us, length us, event | category | flops | bytes accessed | tf_op | source)
XLA Modules:
  0.0 921.1 jit_solution(17429748635721791085)
XLA Ops:
  21.4 48.8 %while.28 = (s32[]{:T(128)}, bf16[4,512,2,64]{1,3,2,0:T(8,128)(2,1)S(1)}, f32[4,2,512]{2,1,0:T(2,128)S(1)}, s32[4]{0:T(128)S(1)}, s32[2048]{0:T(1024)S(1)}, /*in...) while((s32[]{:T(128)}, ...), condition=%wide.region_5.6_spmd.clone, body=%wide.region_2.5_spmd.clone.sunk | while | flops 579862016 | bytes 47633644 | solution.py:63
  27.1 3.2 fusion.131
  30.3 3.2 fusion.132
  39.3 3.2 fusion.131
  42.5 3.2 fusion.132
  51.4 3.2 fusion.131
  54.6 3.2 fusion.132
  63.5 3.2 fusion.131
  66.8 3.2 fusion.132
  70.8 3.3 convolution_convert_fusion.2
  74.8 158.6 %all-reduce.8.cloned.1.call-done = bf16[2048,1024]{1,0:T(8,128)(2,1)} async-done(((bf16[2048,1024]{1,0:T(8,128)(2,1)}), bf16[2048,1024]{1,0:T(8,128)(2,1)}) %all-reduce.8.cloned.1.call-update) | async-done | bytes 4194320 | tf_op jit(solution)/shard_map/psum | solution.py:125
  233.4 5.0 fusion.54
  241.5 3.5 fusion.73
  245.0 6.4 fusion.76
  252.7 4.4 convolution_convert_fusion
  257.8 7.1 convolution_convert_fusion.4
  265.6 4.5 convolution_convert_fusion.5
  270.1 142.6 %all-reduce.10.cloned.1.call-done = bf16[2048,1024]{1,0:T(8,128)(2,1)} async-done(((bf16[2048,1024]{1,0:T(8,128)(2,1)}), bf16[2048,1024]{1,0:T(8,128)(2,1)}) %all-reduce.10.cloned.1.call-update) | async-done | bytes 4194320 | tf_op jit(solution)/shard_map/psum | solution.py:195
  412.7 6.8 fusion.47
  421.0 6.9 fusion.48
  428.0 5.7 fusion.78
  433.6 3.2 copy-done.10
  438.3 5.7 convolution_convert_fusion.3
  445.1 117.2 %while.29 = (s32[]{:T(128)}, f32[2048,2,64]{0,2,1:T(8,128)S(1)}, f32[2048,2,64]{0,2,1:T(8,128)}, bf16[4,512,2,64]{1,3,2,0:T(8,128)(2,1)}, s32[4]{0:T(128)S(1)}, ...) while((s32[]{:T(128)}, f32[2048,2,64]{0,2,1:T(8,128)S(1)}, ...), condition=%wide.region_15.16_spmd.clone, body=%wide.region_13.15_spmd.clone.sunk | while | flops 1371864576 | bytes 145007648 | solution.py:100
  452.2 6.2 multiply_reduce_fusion.3
  458.4 8.8 multiply_convert_fusion.5
  467.2 4.7 fusion.145
  481.7 6.2 multiply_reduce_fusion.3
  487.9 8.8 multiply_convert_fusion.5
  496.7 4.6 fusion.145
  511.0 6.2 multiply_reduce_fusion.3
  517.2 8.7 multiply_convert_fusion.5
  525.9 4.6 fusion.145
  540.2 6.2 multiply_reduce_fusion.3
  546.4 8.7 multiply_convert_fusion.5
  555.1 4.6 fusion.145
  568.1 7.2 convolution_convert_fusion.1
  575.2 4.4 bitcast_convert_fusion
  579.7 3.0 reduce_sum.260
  592.1 3.6 all-gather.3.cloned.1.call-done
  595.7 6.3 reshape.277
  602.0 5.7 reduce_sum.220
  609.0 261.2 %all-reduce.12.cloned.1.call-done = (bf16[2048,1024]{1,0:T(8,128)(2,1)}, bf16[2048,1024]{1,0:T(8,128)(2,1)}) async-done(((bf16[2048,1024]{1,0:T(8,128)(2,1)}, bf16[2048,1024]{1,0:T(8,128)(2,1)}), (bf16[2048,1024]{1,0:T(8,128)(2,1)}, bf16[2048,1024]{1,0:T(8,128)(2,1)})) %all-reduce.12.cloned.1.call-update) | async-done | bytes 8388624 | tf_op jit(solution)/shard_map/psum | solution.py:175
  870.2 4.5 fusion.51
  874.7 2.9 reduce_sum.219
  877.7 6.8 fusion.49
  884.5 10.8 %all-reduce.1 = (bf16[1024]{0:T(1024)(128)(2,1)S(1)}, bf16[1024]{0:T(1024)(128)(2,1)S(1)}, bf16[2,128]{1,0:T(2,128)(2,1)S(1)}, bf16[1024]{0:T(1024)(128)(2,1)S(1...) all-reduce(bf16[1024]{0:T(1024)(128)(2,1)S(1)} %get-tuple-element.2, ...), channel_id=1, replica_groups=mesh['dp'=4,'tensor'=8] {'dp'}, use_global_device_ids=true, to_apply=%region_20.21 | all-reduce | flops 6912 | bytes 27648 | tf_op jit(solution)/shard_map/psum | solution.py:251
  900.0 14.1 %add_convert_fusion = (bf16[2048,1024]{1,0:T(8,128)(2,1)}, bf16[2048,1024]{1,0:T(8,128)(2,1)}) fusion(f32[2048,1024]{1,0:T(8,128)} %copy-done.10, bf16[2048,1024]{1,0:T(8,128)(2,1)} %param.19, bf16[2048,1024]{1,0:T(8,128)(2,1)} %get-tuple-element.260, f32[2048]{0:T(1024)S(1)} %negate_multiply_fusion, f32[2048]{0:T(1024)S(1)} %multiply_multiply_fusion.2, ...), kind=kLoop, calls=%fused_computation.75 | loop fusion | flops 37748736 | bytes 33599488 | tf_op jit(solution)/shard_map/convert_element_type | solution.py:243
  (288 shorter events, 94.2 us)
Async XLA Ops:
  7.2 237.8 %copy-start = (bf16[512,1024]{1,0:T(8,128)(2,1)S(1)}, bf16[512,1024]{1,0:T(8,128)(2,1)}, u32[]{:S(2)}) copy-start(bf16[512,1024]{1,0:T(8,128)(2,1)} %param.31) | copy-start | bytes 3145732
  7.2 226.2 %all-reduce.8.cloned.1.call-start = ((), (), s32[]{:S(2)}) async-start(), calls=%async_computation | async-start | bytes 8388608 | tf_op jit(solution)/shard_map/psum | solution.py:125
  7.3 5.4 copy-start.3
  9.1 5.0 copy-start.35
  21.4 49.3 %copy-start.28 = (bf16[128,1024]{1,0:T(8,128)(2,1)S(1)}, bf16[128,1024]{1,0:T(8,128)(2,1)}, u32[]{:S(2)}) copy-start(bf16[128,1024]{1,0:T(8,128)(2,1)} %param.25) | copy-start | bytes 786436
  70.2 3.9 copy-start.16
  74.1 338.6 %all-reduce.10.cloned.1.call-start = ((), (), s32[]{:S(2)}) async-start(), calls=%async_computation.1 | async-start | bytes 8388608 | tf_op jit(solution)/shard_map/psum | solution.py:195
  74.8 183.0 %copy-start.45 = (f32[512]{0:T(512)}, f32[512]{0:T(512)S(1)}, u32[]{:S(2)}) copy-start(f32[512]{0:T(512)S(1)} %convert_element_type.220) | copy-start | bytes 6148
  74.8 353.2 %copy-start.31 = (f32[1024]{0:T(1024)}, f32[1024]{0:T(1024)S(1)}, u32[]{:S(2)}) copy-start(f32[1024]{0:T(1024)S(1)} %convert_element_type.216) | copy-start | bytes 12292
  233.4 5.0 copy-start.4
  233.4 5.9 copy-start.7
  245.0 6.4 copy-start.54
  257.2 328.6 %all-reduce.14.cloned.1.call-start = ((), (), s32[]{:S(2)}) async-start(), calls=%async_computation.4 | async-start | bytes 4718592 | tf_op jit(solution)/shard_map/psum | solution.py:249
  257.7 7.1 copy-start.5
  257.8 7.1 copy-start.8
  257.8 7.9 copy-start.53
  412.7 6.9 copy-start.6
  412.7 7.1 copy-start.9
  412.7 8.3 copy-start.11
  421.0 6.9 copy-start.15
  427.9 8.9 copy-start.19
  444.0 151.7 %all-gather.3.cloned.1.call-start = ((), (), s32[]{:S(2)}) async-start(), calls=%async_computation.2 | async-start | bytes 3932160 | tf_op jit(solution)/shard_map/all_gather | solution.py:245
  452.2 6.2 copy-start.1
  458.4 8.8 copy-start.12
  467.2 4.8 copy-start.2
  467.2 4.9 copy-start.20
  481.7 6.2 copy-start.1
  487.9 8.8 copy-start.12
  496.7 4.6 copy-start.2
  496.7 4.8 copy-start.20
  511.0 6.2 copy-start.1
  517.2 8.7 copy-start.12
  525.9 4.6 copy-start.2
  525.9 4.8 copy-start.20
  540.2 6.2 copy-start.1
  546.4 8.7 copy-start.12
  555.1 4.6 copy-start.2
  555.1 4.8 copy-start.20
  568.0 7.2 copy-start.51
  568.0 302.2 %all-reduce.12.cloned.1.call-start = ((), (), s32[]{:S(2)}) async-start(), calls=%async_computation.3 | async-start | bytes 16777216 | tf_op jit(solution)/shard_map/psum | solution.py:175
  579.7 5.9 copy-start.22
  585.8 4.7 copy-start.27
  602.0 268.2 %copy-start.30 = (f32[2048]{0:T(1024)S(1)}, f32[2048]{0:T(1024)}, u32[]{:S(2)}) copy-start(f32[2048]{0:T(1024)} %copy-done.29) | copy-start | bytes 24580
  602.0 268.2 %copy-start.36 = (f32[1024]{0:T(1024)S(1)}, f32[1024]{0:T(1024)}, u32[]{:S(2)}) copy-start(f32[1024]{0:T(1024)} %copy-done.35) | copy-start | bytes 12292
  877.6 6.9 copy-start.39
  877.6 6.9 copy-start.40
  877.7 6.8 copy-start.48
  877.7 22.3 %copy-start.32 = (f32[1024]{0:T(1024)S(1)}, f32[1024]{0:T(1024)}, u32[]{:S(2)}) copy-start(f32[1024]{0:T(1024)} %copy-done.31) | copy-start | bytes 12292
  (33 other events, 69.2 us)
Sparse Core Ops, SparseCore 0:
  74.3 159.0 all-reduce.7
  257.3 155.3 all-reduce.9
  444.1 54.6 all-reduce.13
  568.1 27.5 all-gather.2
  600.2 270.0 all-reduce.11
